TPU v7x, 32 devices: a whole 2x2x4 slice. The times are simulated.
32 devices in a mesh: aux: 8 (over y, x, core), orb: 4 (over z).
Axes of the slice: x: 2, y: 2, z: 4, core: 2. Of those that a mesh axis runs over, the one named last changes fastest.
Arguments:
- tiles: float32 [256, 64, 4096], P(('aux', 'orb')), may hold values from -6 to 6
- tile_list: int32 [4, 256], P(None, ('aux', 'orb')), may hold values from 0 to 255, as said below
- orb_factor: float32 [4096, 256], P('orb'), may hold values from -30 to 30
- nu_factor: float32 [512, 256], replicated, may hold values from -30 to 30
Outputs:
- aux_factor: float32 [16384, 256], P('aux')
- orb_updated: float32 [4096, 256], P('orb')
- nu_updated: float32 [512, 256], replicated
Inputs may be any that keep to these rules, and one draw needn't show every extreme that they name: `tile_list`: slot s belongs to the device s // 8 along aux+orb; for that device with aux index a and orb index o, row 0 lies in [a * 32, (a + 1) * 32), row 1 in [o * 16, (o + 1) * 16), row 2 below 8. The coordinates of one device's slots are distinct. Row 3 is 0 or 1: 1 on a device's first slots and 0 on the rest; every device has at least one flagged slot and some device has all 8 flagged.
All inputs are finite; a program needn't handle non-finite values.
Results may differ from a plain program's by a relative error of at most 0.0003.
Values sent between devices are 32-bit elements; how exact they have to be, the bound alone decides.
A program may use at most 256 MiB of HBM per device.

v0:
```python
import jax
import jax.numpy as jnp
from jax import lax
from jax.sharding import PartitionSpec as P

P_SIZE = 16384
MU = 4096
NU = 512


ridge_weight = 0.5
epsilon = 1e-06
highest = lax.Precision.HIGHEST


def gram_of(matrix):
    return jnp.dot(matrix.T, matrix, precision=highest, preferred_element_type=jnp.float32)


def solve_rows(system, targets):
    factor_lower = jnp.linalg.cholesky(system)
    return jax.scipy.linalg.cho_solve((factor_lower, True), targets.T).T


def add_rows(running, addition, start):
    previous = lax.dynamic_slice_in_dim(running, start, addition.shape[0], 0)
    return lax.dynamic_update_slice_in_dim(running, previous + addition, start, 0)


def per_device(tiles, tile_list, orb_factor, nu_factor):
    tile_slots = tiles.shape[0]
    tile_edge = tiles.shape[1]
    rank_width = nu_factor.shape[1]
    first_rows = P_SIZE // lax.axis_size("aux")
    orb_rows = orb_factor.shape[0]
    identity = jnp.eye(rank_width, dtype=jnp.float32)
    first_at = tile_list[0] * tile_edge - lax.axis_index("aux") * first_rows
    second_at = tile_list[1] * tile_edge - lax.axis_index("orb") * orb_rows
    third_at = tile_list[2] * tile_edge
    live_flags = tile_list[3]
    empty_block = jnp.zeros((tile_edge, tile_edge, rank_width), jnp.float32)
    s_nu = gram_of(nu_factor) / NU
    s_orb = lax.psum(gram_of(orb_factor), "orb") / MU
    partial_first = jnp.zeros((first_rows, rank_width), jnp.float32)
    kept_blocks = []
    for tile_slot in range(tile_slots):
        tile_block = tiles[tile_slot]
        nu_block = lax.dynamic_slice_in_dim(nu_factor, third_at[tile_slot], tile_edge, 0)

        def contract_nu(tile_block=tile_block, nu_block=nu_block):
            return jnp.dot(
                tile_block.reshape(tile_edge * tile_edge, tile_edge),
                nu_block,
                precision=highest,
                preferred_element_type=jnp.float32,
            ).reshape(tile_edge, tile_edge, rank_width)

        contracted = lax.cond(live_flags[tile_slot] > 0, contract_nu, lambda: empty_block)
        kept_blocks.append(contracted)
        orb_block = lax.dynamic_slice_in_dim(orb_factor, second_at[tile_slot], tile_edge, 0)
        partial_first = add_rows(
            partial_first, jnp.sum(contracted * orb_block[None], axis=1), first_at[tile_slot]
        )
    system_first = s_orb * s_nu + ridge_weight * identity
    share_first = lax.psum_scatter(partial_first, "orb", scatter_dimension=0, tiled=True)
    a_new = lax.all_gather(solve_rows(system_first, share_first), "orb", axis=0, tiled=True)
    sums_first = lax.psum(jnp.sum(a_new * a_new, axis=0), "aux")
    scale_first = jnp.sqrt(sums_first / P_SIZE + epsilon)
    aux_factor = a_new / scale_first
    s_first = lax.psum(gram_of(aux_factor), "aux") / P_SIZE
    partial_second = jnp.zeros((orb_rows, rank_width), jnp.float32)
    for tile_slot in range(tile_slots):
        aux_block = lax.dynamic_slice_in_dim(aux_factor, first_at[tile_slot], tile_edge, 0)
        addition = jnp.sum(kept_blocks[tile_slot] * aux_block[:, None, :], axis=0)
        partial_second = add_rows(partial_second, addition, second_at[tile_slot])
    system_second = s_first * s_nu + ridge_weight * identity
    share_second = lax.psum_scatter(partial_second, "aux", scatter_dimension=0, tiled=True)
    b_new = lax.all_gather(solve_rows(system_second, share_second), "aux", axis=0, tiled=True)
    sums_second = lax.psum(jnp.sum(b_new * b_new, axis=0), "orb")
    scale_second = jnp.sqrt(sums_second / MU + epsilon)
    orb_updated = b_new / scale_second
    s_second = lax.psum(gram_of(orb_updated), "orb") / MU
    partial_third = jnp.zeros((nu_factor.shape[0], rank_width), jnp.float32)
    for tile_slot in range(tile_slots):
        tile_block = tiles[tile_slot]
        aux_block = lax.dynamic_slice_in_dim(aux_factor, first_at[tile_slot], tile_edge, 0)

        def contract_aux(tile_block=tile_block, aux_block=aux_block):
            return lax.dot_general(
                tile_block,
                aux_block,
                (((0,), (0,)), ((), ())),
                precision=highest,
                preferred_element_type=jnp.float32,
            ).reshape(tile_edge, tile_edge, rank_width)

        contracted = lax.cond(live_flags[tile_slot] > 0, contract_aux, lambda: empty_block)
        orb_block = lax.dynamic_slice_in_dim(orb_updated, second_at[tile_slot], tile_edge, 0)
        partial_third = add_rows(
            partial_third, jnp.sum(contracted * orb_block[:, None, :], axis=0), third_at[tile_slot]
        )
    summed_third = lax.psum(partial_third, ("aux", "orb"))
    c_new = solve_rows(s_first * s_second + ridge_weight * identity, summed_third)
    scale_third = jnp.sqrt(jnp.sum(c_new * c_new, axis=0) / NU + epsilon)
    nu_updated = c_new / scale_third
    return (aux_factor, orb_updated, nu_updated)


def solution(mesh):
    return jax.shard_map(
        per_device,
        mesh=mesh,
        in_specs=(P(("aux", "orb"), None, None), P(None, ("aux", "orb")), P("orb", None), P()),
        out_specs=(P("aux", None), P("orb", None), P()),
        check_vma=False,
    )
```

profile of v0, /device:TPU:0, one launch (start us, length us, event | category | flops | bytes accessed | tf_op | source)
XLA Modules:
  0.0 717.4 jit_solution(1320075898996524115)
XLA Ops:
  44.4 6.2 fusion.76
  60.3 10.8 %conditional.16 = (f32[64,64,256]{2,1,0:T(8,128)}) conditional(s32[]{:T(128)} %bitcast.60, () %tuple.122, (f32[512,256]{1,0:T(8,128)}, s32[]{:T(128)}, f32[1,64,4096]{1,2,0:T(8,128)}) %tuple.123), branch_computations={%region_5.7_spmd, %region_6.8_spmd} | conditional | flops 805306368 | bytes 8454664 | solution.py:58
  64.2 7.0 convolution_bitcast_fusion
  76.0 9.9 %conditional.17 = (f32[64,64,256]{2,1,0:T(8,128)}) conditional(s32[]{:T(128)} %bitcast.65, () %tuple.124, (f32[512,256]{1,0:T(8,128)S(1)}, s32[]{:T(128)}, f32[1,64,4096]{1,2,0:T(8,128)S(1)}) %tuple.350), branch_computations={%region_8.10_spmd, %region_9.11_spmd} | conditional | flops 805306368 | bytes 7405580 | solution.py:58
  78.9 7.0 convolution_bitcast_fusion.1
  95.0 10.8 %conditional.18 = (f32[64,64,256]{2,1,0:T(8,128)}) conditional(s32[]{:T(128)} %bitcast.69, () %tuple.126, (f32[512,256]{1,0:T(8,128)S(1)}, s32[]{:T(128)}, f32[1,64,4096]{1,2,0:T(8,128)}) %tuple.351), branch_computations={%region_11.13_spmd, %region_12.14_spmd} | conditional | flops 805306368 | bytes 7405580 | solution.py:58
  98.8 7.0 convolution_bitcast_fusion.2
  172.8 11.7 %cholesky.172 = f32[128,128]{1,0:T(8,128)S(1)} custom-call(f32[128,128]{1,0:T(8,128)S(1)} %cholesky.270), custom_call_target="Cholesky" | custom-call | tf_op jit(solution)/shard_map/jit(cholesky)/cholesky | solution.py:21
  184.5 9.8 %custom-call.24 = f32[1,128,128]{1,2,0:T(8,128)S(1)} custom-call(f32[1,128,128]{2,1,0:T(8,128)S(1)} %get-tuple-element.387), custom_call_target="InvertDiagBlocksLowerTriangular" | custom-call | tf_op jit(solution)/shard_map/jit(cholesky)/cholesky | solution.py:21
  194.9 11.7 %cholesky.189 = f32[128,128]{1,0:T(8,128)S(1)} custom-call(f32[128,128]{1,0:T(8,128)S(1)} %convolution_subtract_fusion.8), custom_call_target="Cholesky" | custom-call | tf_op jit(solution)/shard_map/jit(cholesky)/cholesky | solution.py:21
  212.8 19.7 %custom-call.25 = f32[2,128,128]{1,2,0:T(8,128)S(1)} custom-call(f32[2,128,128]{2,1,0:T(8,128)S(1)} %get-tuple-element.267), custom_call_target="InvertDiagBlocksLowerTriangular" | custom-call | tf_op jit(solution)/shard_map/jit(_cho_solve)/triangular_solve | solution.py:22
  232.5 23.3 %reduce-scatter.3.cloned.1.call-done = f32[512,256]{1,0:T(8,128)} async-done(((f32[2048,256]{1,0:T(8,128)}), f32[512,256]{1,0:T(8,128)}) %reduce-scatter.3.cloned.1.call-update) | async-done | bytes 524304 | tf_op jit(solution)/shard_map/reduce_scatter | solution.py:65
  261.2 65.1 %all-gather.3.cloned.1.call-done = f32[2048,256]{0,1:T(8,128)} async-done(((f32[512,256]{0,1:T(8,128)}), f32[2048,256]{0,1:T(8,128)}) %all-gather.3.cloned.1.call-update) | async-done | bytes 2097168 | tf_op jit(solution)/shard_map/all_gather | solution.py:66
  328.0 13.4 %psum.43 = f32[256]{0:T(256)S(1)} all-reduce(f32[256]{0:T(256)S(1)} %multiply_reduce_fusion.24), channel_id=1, replica_groups=mesh['aux'=8,'orb'=4] {'aux'}, use_global_device_ids=true, to_apply=%region_31.0 | all-reduce | flops 256 | bytes 2048 | tf_op jit(solution)/shard_map/psum | solution.py:67
  391.9 5.7 all-reduce.8.cloned.1.call-done
  398.9 11.7 %cholesky.206 = f32[128,128]{1,0:T(8,128)S(1)} custom-call(f32[128,128]{1,0:T(8,128)S(1)} %cholesky.273), custom_call_target="Cholesky" | custom-call | tf_op jit(solution)/shard_map/jit(cholesky)/cholesky | solution.py:21
  410.7 9.8 %custom-call.26 = f32[1,128,128]{1,2,0:T(8,128)S(1)} custom-call(f32[1,128,128]{2,1,0:T(8,128)S(1)} %get-tuple-element.383), custom_call_target="InvertDiagBlocksLowerTriangular" | custom-call | tf_op jit(solution)/shard_map/jit(cholesky)/cholesky | solution.py:21
  421.0 11.7 %cholesky.223 = f32[128,128]{1,0:T(8,128)S(1)} custom-call(f32[128,128]{1,0:T(8,128)S(1)} %convolution_subtract_fusion.7), custom_call_target="Cholesky" | custom-call | tf_op jit(solution)/shard_map/jit(cholesky)/cholesky | solution.py:21
  440.4 19.7 %custom-call.20 = f32[2,128,128]{1,2,0:T(8,128)S(1)} custom-call(f32[2,128,128]{2,1,0:T(8,128)S(1)} %get-tuple-element.260), custom_call_target="InvertDiagBlocksLowerTriangular" | custom-call | tf_op jit(solution)/shard_map/jit(_cho_solve)/triangular_solve | solution.py:22
  478.6 7.1 conditional.26
  478.6 7.1 fusion.28
  485.8 5.1 conditional.25
  485.9 5.0 fusion.26
  490.9 6.9 conditional.24
  490.9 6.9 fusion.24
  499.2 34.6 %psum.45 = f32[256]{0:T(256)S(1)} all-reduce(f32[256]{0:T(256)S(1)} %multiply_reduce_fusion.25), channel_id=1, replica_groups=mesh['aux'=8,'orb'=4] {'orb'}, use_global_device_ids=true, to_apply=%region_43.46 | all-reduce | flops 256 | bytes 2048 | tf_op jit(solution)/shard_map/psum | solution.py:79
  563.8 5.2 all-reduce.10.cloned.1.call-done
  570.2 11.7 %cholesky.240 = f32[128,128]{1,0:T(8,128)S(1)} custom-call(f32[128,128]{1,0:T(8,128)S(1)} %cholesky.276), custom_call_target="Cholesky" | custom-call | tf_op jit(solution)/shard_map/jit(cholesky)/cholesky | solution.py:21
  581.9 9.8 %custom-call.27 = f32[1,128,128]{1,2,0:T(8,128)S(1)} custom-call(f32[1,128,128]{2,1,0:T(8,128)S(1)} %get-tuple-element.381), custom_call_target="InvertDiagBlocksLowerTriangular" | custom-call | tf_op jit(solution)/shard_map/jit(cholesky)/cholesky | solution.py:21
  592.2 11.7 %cholesky.257 = f32[128,128]{1,0:T(8,128)S(1)} custom-call(f32[128,128]{1,0:T(8,128)S(1)} %convolution_subtract_fusion.4), custom_call_target="Cholesky" | custom-call | tf_op jit(solution)/shard_map/jit(cholesky)/cholesky | solution.py:21
  610.7 19.9 %custom-call.28 = f32[2,128,128]{1,2,0:T(8,128)S(1)} custom-call(f32[2,128,128]{2,1,0:T(8,128)S(1)} %get-tuple-element.268), custom_call_target="InvertDiagBlocksLowerTriangular" | custom-call | tf_op jit(solution)/shard_map/jit(_cho_solve)/triangular_solve | solution.py:22
  630.7 73.6 %all-reduce.12.cloned.1.call-done = f32[256,512]{0,1:T(8,128)} async-done(((f32[256,512]{0,1:T(8,128)}), f32[256,512]{0,1:T(8,128)}) %all-reduce.12.cloned.1.call-update) | async-done | bytes 524304 | tf_op jit(solution)/shard_map/psum | solution.py:102
  (302 shorter events, 257.4 us)
Async XLA Ops:
  7.2 162.7 %all-reduce.6.cloned.1.call-start = ((), (), s32[]{:S(2)}) async-start(), calls=%async_computation.2 | async-start | bytes 524288 | tf_op jit(solution)/shard_map/psum | solution.py:43
  11.3 244.4 %reduce-scatter.3.cloned.1.call-start = ((), (), s32[]{:S(2)}) async-start(), calls=%async_computation.3 | async-start | bytes 2621440 | tf_op jit(solution)/shard_map/reduce_scatter | solution.py:65
  53.8 22.2 %copy-start = (f32[1,64,4096]{1,2,0:T(8,128)}, f32[1,64,4096]{1,2,0:T(8,128)S(1)}, u32[]{:S(2)}) copy-start(f32[1,64,4096]{1,2,0:T(8,128)S(1)} %copy.91) | copy-start | bytes 3145732
  60.3 10.8 %copy-start.6 = (f32[1024,256]{1,0:T(8,128)S(1)}, f32[1024,256]{1,0:T(8,128)}, u32[]{:S(2)}) copy-start(f32[1024,256]{1,0:T(8,128)} %param.41) | copy-start | bytes 3145732
  71.8 4.2 copy-start.8
  76.0 9.9 %copy-start.25 = (f32[64,256]{1,0:T(8,128)S(1)}, f32[64,256]{1,0:T(8,128)}, u32[]{:S(2)}) copy-start(f32[64,256]{1,0:T(8,128)} %get-tuple-element.375) | copy-start | bytes 196612
  143.1 4.6 copy-start.5
  149.6 7.9 %copy-start.2 = (f32[1,64,4096]{1,2,0:T(8,128)}, f32[1,64,4096]{1,2,0:T(8,128)S(1)}, u32[]{:S(2)}) copy-start(f32[1,64,4096]{1,2,0:T(8,128)S(1)} %copy.97) | copy-start | bytes 3145732
  169.4 156.8 %all-gather.3.cloned.1.call-start = ((), (), s32[]{:S(2)}) async-start(), calls=%async_computation.4 | async-start | bytes 2621440 | tf_op jit(solution)/shard_map/all_gather | solution.py:66
  261.1 136.5 %all-reduce.8.cloned.1.call-start = ((), (), s32[]{:S(2)}) async-start(), calls=%async_computation.5 | async-start | bytes 524288 | tf_op jit(solution)/shard_map/psum | solution.py:70
  346.3 6.9 copy-start.18
  346.3 6.9 copy-start.20
  346.3 6.9 copy-start.16
  346.3 10.2 %copy-start.14 = (f32[64,256]{0,1:T(8,128)}, f32[64,256]{0,1:T(8,128)S(1)}, u32[]{:S(2)}) copy-start(f32[64,256]{0,1:T(8,128)S(1)} %get-tuple-element.357) | copy-start | bytes 196612
  346.3 13.5 %copy-start.12 = (f32[64,256]{0,1:T(8,128)}, f32[64,256]{0,1:T(8,128)S(1)}, u32[]{:S(2)}) copy-start(f32[64,256]{0,1:T(8,128)S(1)} %get-tuple-element.358) | copy-start | bytes 196612
  346.3 16.9 %copy-start.10 = (f32[64,256]{0,1:T(8,128)}, f32[64,256]{0,1:T(8,128)S(1)}, u32[]{:S(2)}) copy-start(f32[64,256]{0,1:T(8,128)S(1)} %get-tuple-element.359) | copy-start | bytes 196612
  346.4 113.7 %reduce-scatter.5.cloned.1.call-start = ((), (), s32[]{:S(2)}) async-start(), calls=%async_computation.6 | async-start | bytes 1179648 | tf_op jit(solution)/shard_map/reduce_scatter | solution.py:77
  369.9 18.5 %copy-start.24 = (f32[64,256]{1,0:T(8,128)S(1)}, f32[64,256]{1,0:T(8,128)}, u32[]{:S(2)}) copy-start(f32[64,256]{1,0:T(8,128)} %multiply_reduce_fusion.9) | copy-start | bytes 196612
  369.9 20.3 %copy-start.23 = (f32[64,256]{1,0:T(8,128)S(1)}, f32[64,256]{1,0:T(8,128)}, u32[]{:S(2)}) copy-start(f32[64,256]{1,0:T(8,128)} %multiply_reduce_fusion.8) | copy-start | bytes 196612
  391.9 106.0 %all-gather.5.cloned.1.call-start = ((), (), s32[]{:S(2)}) async-start(), calls=%async_computation.7 | async-start | bytes 1179648 | tf_op jit(solution)/shard_map/all_gather | solution.py:78
  397.6 66.4 %copy-start.21 = (f32[64,256]{0,1:T(8,128)S(1)}, f32[64,256]{0,1:T(8,128)}, u32[]{:S(2)}) copy-start(f32[64,256]{0,1:T(8,128)} %copy-done.20) | copy-start | bytes 196612
  464.0 105.0 %all-reduce.10.cloned.1.call-start = ((), (), s32[]{:S(2)}) async-start(), calls=%async_computation.8 | async-start | bytes 524288 | tf_op jit(solution)/shard_map/psum | solution.py:82
  465.8 2.5 copy-start.19
  468.3 2.5 copy-start.17
  470.8 2.9 copy-start.15
  473.7 2.5 copy-start.13
  476.1 2.5 copy-start.11
  478.6 7.1 copy-start.1
  537.3 167.1 %all-reduce.12.cloned.1.call-start = ((), (), s32[]{:S(2)}) async-start(), calls=%async_computation.9 | async-start | bytes 1048576 | tf_op jit(solution)/shard_map/psum | solution.py:102
  538.0 3.5 copy-start.4
  556.2 3.5 copy-start.3
  559.7 9.3 %copy-start.22 = (f32[256,256]{0,1:T(8,128)S(1)}, f32[256,256]{0,1:T(8,128)}, u32[]{:S(2)}) copy-start(f32[256,256]{0,1:T(8,128)} %all-reduce.8.cloned.1.call-done) | copy-start | bytes 786436
  (2 other events, 1.8 us)
Sparse Core Ops, SparseCore 0:
  11.4 38.3 all-reduce.5
  169.5 86.1 reduce-scatter.2
  261.2 64.9 all-gather.2
  346.5 51.0 all-reduce.7
  401.2 35.5 reduce-scatter.4
  464.1 22.8 all-gather.4
  537.4 31.5 all-reduce.9
  574.8 129.4 all-reduce.11
where the time goes:
time: 728 us; the launch traced here: 717 us
  other arithmetic  250 us (34%)
  waiting for transfers between devices  173 us (24%)
  local copies, waits for them, and re-layouts  108 us (15%)
  between operations  70.4 us (10%)
  matrix products  64.5 us (9%)
  blocking collectives  48 us (7%)
    another operation x20, other arithmetic, solve_rows(): factor_lower = jnp.linalg.cholesky(system)  103 us
    psum x1, waiting for transfers between devices, per_device(): summed_third = lax.psum(partial_third, ('aux', 'orb'))  73.6 us
    all_gather x1, waiting for transfers between devices, per_device(): lax.all_gather(solve_rows(system_first, share_first), 'orb', axis=0, tile...  65.1 us
    another operation x7, other arithmetic, solve_rows(): return jax.scipy.linalg.cho_solve((factor_lower, True), targets.T).T  59.4 us
    psum x1, blocking collectives, per_device(): sums_second = lax.psum(jnp.sum(b_new * b_new, axis=0), 'orb')  34.6 us
    unnamed x63, local copies, waits for them, and re-layouts  28.1 us
    reduce_sum x8, other arithmetic, per_device(): addition = jnp.sum(kept_blocks[tile_slot] * aux_block[:, None, :], axis=0)  26.1 us
    broadcast_in_dim x10, local copies, waits for them, and re-layouts, per_device(): empty_block = jnp.zeros((tile_edge, tile_edge, rank_width), jnp.float32)  24.7 us
  transfers between devices with their start and end apart: 8, of which 5 were waited for; matrix products, arithmetic and copies ran while one was open for 54% of the time, Pallas kernels for 0%

commit v1 on v0

v1 whole, which is shorter than its diff:
```python
import functools

import jax
import jax.numpy as jnp
from jax import lax
from jax.experimental import pallas as pl
from jax.experimental.pallas import tpu as pltpu
from jax.sharding import PartitionSpec as P

P_SIZE = 16384
MU = 4096
NU = 512

ridge_weight = 0.5
epsilon = 1e-06
highest = lax.Precision.HIGHEST
f32 = jnp.float32
bf16 = jnp.bfloat16
PANEL = 32


def gram_of(matrix):
    return jnp.dot(matrix.T, matrix, precision=highest, preferred_element_type=f32)


def split_two(x):
    high = x.astype(bf16)
    return high, (x - high.astype(f32)).astype(bf16)


def split_three(x):
    high = x.astype(bf16)
    rest = x - high.astype(f32)
    middle = rest.astype(bf16)
    return high, middle, (rest - middle.astype(f32)).astype(bf16)


def first_kernel(edge, index_ref, x_ref, orb_ref, nu_ref, out_ref):
    slot = pl.program_id(0)
    second_at = pl.multiple_of(index_ref[1, slot] * edge, edge)
    third_at = pl.multiple_of(index_ref[2, slot] * edge, edge)
    nu_block = nu_ref[pl.ds(third_at, edge), :]
    orb_block = orb_ref[pl.ds(second_at, edge), :]
    rank = nu_block.shape[1]
    group = 4
    total = jnp.zeros((edge, rank), f32)
    for start in range(0, edge, group):
        x_high, x_low = split_two(x_ref[0, :, start * edge:(start + group) * edge])
        stacked = jnp.concatenate([x_high, x_low], axis=0)
        product = jnp.concatenate(
            [nu_block * orb_block[j:j + 1, :] for j in range(start, start + group)], axis=0
        )
        high, low = split_two(product)
        main = jnp.dot(stacked, high, preferred_element_type=f32)
        rest = jnp.dot(x_high, low, preferred_element_type=f32)
        total += main[:edge] + (main[edge:] + rest)
    out_ref[...] = jnp.where(index_ref[3, slot] > 0, total, 0.0)


def solve_kernel(edge, blocks, at_ref, part_ref, inverse_ref, a_ref, gram_ref, total_ref):
    total_ref[...] = jnp.zeros_like(total_ref)

    def add_block(block, carry):
        rows = pl.ds(pl.multiple_of(at_ref[block] * edge, edge), edge)
        total_ref[rows, :] += part_ref[pl.ds(pl.multiple_of(block * edge, edge), edge), :]
        return carry

    lax.fori_loop(0, blocks, add_block, 0)
    inverse = inverse_ref[...]
    chunk = min(256, total_ref.shape[0])
    gram_ref[...] = jnp.zeros_like(gram_ref)

    def apply(step, carry):
        rows = pl.ds(pl.multiple_of(step * chunk, chunk), chunk)
        solved = jnp.dot(total_ref[rows, :], inverse, precision=highest, preferred_element_type=f32)
        a_ref[rows, :] = solved
        gram_ref[...] += lax.dot_general(
            solved, solved, (((0,), (0,)), ((), ())), precision=highest, preferred_element_type=f32
        )
        return carry

    lax.fori_loop(0, total_ref.shape[0] // chunk, apply, 0)


def second_kernel(edge, index_ref, x_ref, a_ref, nu_ref, e_ref, out_ref):
    slot = pl.program_id(0)
    first_at = pl.multiple_of(index_ref[0, slot] * edge, edge)
    second_at = pl.multiple_of(index_ref[1, slot] * edge, edge)
    third_at = pl.multiple_of(index_ref[2, slot] * edge, edge)
    live = index_ref[3, slot] > 0

    @pl.when(slot == 0)
    def _():
        out_ref[...] = jnp.zeros_like(out_ref)

    nu_block = nu_ref[pl.ds(third_at, edge), :]
    a_high, a_low = split_two(a_ref[pl.ds(first_at, edge), :])
    weights = jnp.concatenate([a_high, a_high, a_low, a_low], axis=0)
    group = 8
    for start in range(0, edge, group):
        x_high, x_low = split_two(x_ref[0, :, start * edge:(start + group) * edge])
        turned = jnp.concatenate([x_high, x_low], axis=0).T
        e = jnp.dot(
            jnp.concatenate([turned, turned], axis=1), weights, preferred_element_type=f32
        )
        e_ref[0, start * edge:(start + group) * edge, :] = e
        sums = jnp.sum(e.reshape(group, edge, e.shape[1]) * nu_block[None], axis=1)
        rows = pl.ds(pl.multiple_of(second_at + start, group), group)
        out_ref[rows, :] += jnp.where(live, sums, 0.0)


def third_kernel(edge, index_ref, e_ref, b_ref, out_ref):
    slot = pl.program_id(0)
    second_at = pl.multiple_of(index_ref[1, slot] * edge, edge)
    third_at = pl.multiple_of(index_ref[2, slot] * edge, edge)

    @pl.when(slot == 0)
    def _():
        out_ref[...] = jnp.zeros_like(out_ref)

    b_block = b_ref[pl.ds(second_at, edge), :]
    total = jnp.zeros((edge, b_block.shape[1]), f32)
    for j in range(edge):
        total += e_ref[0, j * edge:(j + 1) * edge, :] * b_block[j:j + 1, :]
    out_ref[pl.ds(third_at, edge), :] += jnp.where(index_ref[3, slot] > 0, total, 0.0)


def eye_mask(n):
    return lax.broadcasted_iota(jnp.int32, (n, n), 0) == lax.broadcasted_iota(jnp.int32, (n, n), 1)


def unit_gram(gram, rows):
    diagonal = jnp.where(eye_mask(gram.shape[0]), gram, 0.0)
    along = jnp.sqrt(jnp.sum(diagonal, axis=0, keepdims=True) / rows + epsilon)
    down = jnp.sqrt(jnp.sum(diagonal, axis=1, keepdims=True) / rows + epsilon)
    return gram / down / along / rows, along


def sweep_inverse(a_ref):
    n = a_ref.shape[0]
    lane = lax.broadcasted_iota(jnp.int32, (PANEL, n), 1)
    row = lax.broadcasted_iota(jnp.int32, (PANEL, n), 0)

    def panel_step(step, carry):
        before = a_ref[:PANEL, :]
        panel = before
        for k in range(0, PANEL, 2):
            first = jnp.broadcast_to(panel[:, k:k + 1], panel.shape)
            second = jnp.broadcast_to(panel[:, k + 1:k + 2], panel.shape)
            at_first, at_second = lane == k, lane == k + 1
            unit_first = jnp.where(at_second[:1], 0.0, panel[k:k + 1, :])
            unit_first = jnp.where(at_first[:1], 1.0, unit_first)
            unit_second = jnp.where(at_first[:1], 0.0, panel[k + 1:k + 2, :])
            unit_second = jnp.where(at_second[:1], 1.0, unit_second)
            inverse = 1.0 / first[k:k + 1, :]
            across = second[k:k + 1, :]
            factor = first[k + 1:k + 2, :] * inverse
            inverse_schur = 1.0 / (second[k + 1:k + 2, :] - factor * across)
            new_second = (unit_second - factor * unit_first) * inverse_schur
            new_first = (unit_first - across * new_second) * inverse
            kept = jnp.where(at_first | at_second, 0.0, panel)
            panel = kept - first * new_first - second * new_second
            panel = jnp.where(row == k, new_first, jnp.where(row == k + 1, new_second, panel))
        own = lane < PANEL
        update = jnp.where(own, -panel, panel)
        w_high, w_middle, w_low = split_three(before)
        z_high, z_middle, z_low = split_three(update)
        left = jnp.concatenate([w_low, w_middle, w_high, w_middle, w_high, w_high], axis=0)
        right = jnp.concatenate([z_high, z_middle, z_low, z_high, z_middle, z_high], axis=0)
        change = lax.dot_general(
            left, right, (((0,), (0,)), ((), ())), preferred_element_type=f32
        )
        others = jnp.where(own[:1], 0.0, a_ref[PANEL:, :]) - change[PANEL:, :]
        a_ref[:n - PANEL, :] = pltpu.roll(others, n - PANEL, 1)
        a_ref[n - PANEL:, :] = pltpu.roll(update, n - PANEL, 1)
        return carry

    lax.fori_loop(0, n // PANEL, panel_step, 0)


def inverse_kernel(left_rows, right_rows, left_ref, right_ref, inverse_ref, scale_ref, a_ref):
    left = left_ref[...]
    if left_rows:
        left, scale_ref[...] = unit_gram(left, left_rows)
    else:
        scale_ref[...] = jnp.ones_like(scale_ref)
    right = right_ref[...]
    if right_rows:
        right, _ = unit_gram(right, right_rows)
    n = left.shape[0]
    a_ref[...] = left * right + jnp.where(eye_mask(n), ridge_weight, 0.0)
    sweep_inverse(a_ref)
    inverse_ref[...] = -a_ref[...]


def inverse_of(left, right, left_rows, right_rows, name):
    n = left.shape[0]
    whole = pl.BlockSpec(memory_space=pltpu.VMEM)
    return pl.pallas_call(
        functools.partial(inverse_kernel, left_rows, right_rows),
        out_shape=(jax.ShapeDtypeStruct((n, n), f32), jax.ShapeDtypeStruct((1, n), f32)),
        in_specs=[whole, whole],
        out_specs=(whole, whole),
        scratch_shapes=[pltpu.VMEM((n, n), f32)],
        compiler_params=pltpu.CompilerParams(vmem_limit_bytes=16 << 20),
        cost_estimate=pl.CostEstimate(flops=10**9, bytes_accessed=4 * n * n * 4, transcendentals=0),
        name=name,
    )(left, right)


def per_device(tiles, tile_list, orb_factor, nu_factor):
    slots, edge = tiles.shape[0], tiles.shape[1]
    rank = nu_factor.shape[1]
    first_rows = P_SIZE // lax.axis_size("aux")
    orb_rows = orb_factor.shape[0]
    orb_size = lax.axis_size("orb")
    tile_width = tiles.shape[2]
    index = tile_list - jnp.stack(
        [
            lax.axis_index("aux") * (first_rows // edge),
            lax.axis_index("orb") * (orb_rows // edge),
            jnp.int32(0),
            jnp.int32(0),
        ]
    ).astype(jnp.int32)[:, None]
    tile_spec = pl.BlockSpec((1, edge, tile_width), lambda s, i: (s, 0, 0))

    def full(rows):
        return pl.BlockSpec((rows, rank), lambda s, i: (0, 0))

    own_row = lax.broadcasted_iota(jnp.int32, (orb_size, slots), 0) == lax.axis_index("orb")
    own_at = jnp.where(own_row, index[0].astype(f32)[None], 0.0)
    s_nu = gram_of(nu_factor) / NU
    gram_orb, slot_at = lax.psum((gram_of(orb_factor), own_at), "orb")
    s_orb = gram_orb / MU
    slot_at = slot_at.astype(jnp.int32).reshape(-1)

    parts = pl.pallas_call(
        functools.partial(first_kernel, edge),
        out_shape=jax.ShapeDtypeStruct((slots * edge, rank), f32),
        grid_spec=pltpu.PrefetchScalarGridSpec(
            num_scalar_prefetch=1,
            grid=(slots,),
            in_specs=[tile_spec, full(orb_rows), full(nu_factor.shape[0])],
            out_specs=pl.BlockSpec((edge, rank), lambda s, i: (s, 0)),
        ),
        name="mode_first",
    )(index, tiles, orb_factor, nu_factor)
    gathered = lax.all_gather(parts, "orb", axis=0, tiled=True)
    inverse_first, _ = inverse_of(s_orb, s_nu, 0, 0, "inverse_first")
    blocks = slots * orb_size
    vmem = pl.BlockSpec(memory_space=pltpu.VMEM)
    a_new, gram_a = pl.pallas_call(
        functools.partial(solve_kernel, edge, blocks),
        out_shape=(
            jax.ShapeDtypeStruct((first_rows, rank), f32),
            jax.ShapeDtypeStruct((rank, rank), f32),
        ),
        in_specs=[pl.BlockSpec(memory_space=pltpu.SMEM), vmem, vmem],
        out_specs=(vmem, vmem),
        scratch_shapes=[pltpu.VMEM((first_rows, rank), f32)],
        name="solve_first",
    )(slot_at, gathered, inverse_first)
    gram_a = lax.psum(gram_a, "aux")

    e_all, partial_second = pl.pallas_call(
        functools.partial(second_kernel, edge),
        out_shape=(
            jax.ShapeDtypeStruct((slots, tile_width, rank), f32),
            jax.ShapeDtypeStruct((orb_rows, rank), f32),
        ),
        grid_spec=pltpu.PrefetchScalarGridSpec(
            num_scalar_prefetch=1,
            grid=(slots,),
            in_specs=[tile_spec, full(first_rows), full(nu_factor.shape[0])],
            out_specs=(
                pl.BlockSpec((1, tile_width, rank), lambda s, i: (s, 0, 0)),
                full(orb_rows),
            ),
        ),
        name="mode_second",
    )(index, tiles, a_new, nu_factor)
    sums_first = jnp.sum(jnp.where(eye_mask(rank), gram_a, 0.0), axis=0)
    scale_first = jnp.sqrt(sums_first / P_SIZE + epsilon)
    second_sums = lax.psum(partial_second / scale_first, "aux")
    inverse_second, _ = inverse_of(gram_a, s_nu, P_SIZE, 0, "inverse_second")
    aux_factor = a_new / scale_first
    b_new = jnp.dot(second_sums, inverse_second, precision=highest, preferred_element_type=f32)
    gram_b = lax.psum(gram_of(b_new), "orb")

    partial_third = pl.pallas_call(
        functools.partial(third_kernel, edge),
        out_shape=jax.ShapeDtypeStruct((nu_factor.shape[0], rank), f32),
        grid_spec=pltpu.PrefetchScalarGridSpec(
            num_scalar_prefetch=1,
            grid=(slots,),
            in_specs=[
                pl.BlockSpec((1, tile_width, rank), lambda s, i: (s, 0, 0)),
                full(orb_rows),
            ],
            out_specs=full(nu_factor.shape[0]),
        ),
        name="mode_third",
    )(index, e_all, b_new)
    third_sums = lax.psum(partial_third, ("aux", "orb"))
    inverse_third, scale_second = inverse_of(gram_b, gram_a, MU, P_SIZE, "inverse_third")
    orb_updated = b_new / scale_second
    c_new = jnp.dot(
        third_sums / scale_first / scale_second,
        inverse_third,
        precision=highest,
        preferred_element_type=f32,
    )
    scale_third = jnp.sqrt(jnp.sum(c_new * c_new, axis=0) / NU + epsilon)
    nu_updated = c_new / scale_third
    return (aux_factor, orb_updated, nu_updated)


def solution(mesh):
    return jax.shard_map(
        per_device,
        mesh=mesh,
        in_specs=(P(("aux", "orb"), None, None), P(None, ("aux", "orb")), P("orb", None), P()),
        out_specs=(P("aux", None), P("orb", None), P()),
        check_vma=False,
    )
```

time: 728 us -> 407 us (0.56); the launches traced: 717 us -> 406 us
  other arithmetic: 250 us -> 9.19 us
  Pallas kernels: 0 us -> 106 us
  local copies, waits for them, and re-layouts: 108 us -> 2.36 us
  waiting for transfers between devices: 173 us -> 250 us
  between operations: 70.4 us -> 14.2 us
  matrix products: 64.5 us -> 11.5 us
  blocking collectives: 48 us -> 13.5 us
    another operation x27 -> x2, other arithmetic: 163 us -> 0.09 us  [the longest x1 0.08 us: per_device(): jnp.stack([lax.axis_index('aux') * (first_rows // edge), lax.axis_index('...]
    psum x4 -> x5, waiting for transfers between devices: 84.6 us -> 220 us  [the longest x1 116 us: per_device(): third_sums = lax.psum(partial_third, ('aux', 'orb'))]
    pallas_call x0 -> x7, Pallas kernels: none -> 106 us  [the longest x3 50.1 us: inverse_of(): pl.pallas_call(functools.partial(inverse_kernel, left_rows, right_rows),...]
    reduce_sum x27 -> x1, other arithmetic: 69.5 us -> 1.06 us  [per_device(): sums_first = jnp.sum(jnp.where(eye_mask(rank), gram_a, 0.0), axis=0)]
    dot_general x10 -> x5, matrix products: 51 us -> 11.5 us  [the longest x3 7.67 us: gram_of(): jnp.dot(matrix.T, matrix, precision=highest, preferred_element_type=f32)]
    all_gather x2 -> x1, waiting for transfers between devices: 65.1 us -> 29.6 us  [per_device(): gathered = lax.all_gather(parts, 'orb', axis=0, tiled=True)]
    psum x2 -> x1, blocking collectives: 48 us -> 13.5 us  [per_device(): gram_orb, slot_at = lax.psum((gram_of(orb_factor), own_at), 'orb')]
    unnamed x63 -> x16, local copies, waits for them, and re-layouts: 28.1 us -> 1.68 us
  transfers between devices with their start and end apart: 8 -> 6, of which waited for: 5 -> 6; matrix products, arithmetic and copies ran while one was open for 54% -> 2% of each run, Pallas kernels for 0% -> 23%
where the time goes in v1:
time: 407 us; the launch traced here: 406 us
  waiting for transfers between devices  250 us (61%)
  Pallas kernels  106 us (26%)
  between operations  14.2 us (3%)
  blocking collectives  13.5 us (3%)
  matrix products  11.5 us (3%)
  other arithmetic  9.19 us (2%)
    psum x1, waiting for transfers between devices, per_device(): third_sums = lax.psum(partial_third, ('aux', 'orb'))  116 us
    pallas_call x3, Pallas kernels, inverse_of(): pl.pallas_call(functools.partial(inverse_kernel, left_rows, right_rows),...  50.1 us
    psum x1, waiting for transfers between devices, per_device(): second_sums = lax.psum(partial_second / scale_first, 'aux')  39.6 us
    psum x1, waiting for transfers between devices, per_device(): gram_a = lax.psum(gram_a, 'aux')  35.7 us
    all_gather x1, waiting for transfers between devices, per_device(): gathered = lax.all_gather(parts, 'orb', axis=0, tiled=True)  29.6 us
    psum x1, waiting for transfers between devices, per_device(): gram_b = lax.psum(gram_of(b_new), 'orb')  19.2 us
    pallas_call x1, Pallas kernels, per_device(): pl.pallas_call(functools.partial(second_kernel, edge), out_shape=(jax.Sha...  16.9 us
    pallas_call x1, Pallas kernels, per_device(): pl.pallas_call(functools.partial(third_kernel, edge), out_shape=jax.Shape...  14.2 us
  transfers between devices with their start and end apart: 6, of which 6 were waited for; matrix products, arithmetic and copies ran while one was open for 2% of the time, Pallas kernels for 23%

profile of v1, /device:TPU:0, one launch (start us, length us, event | category | flops | bytes accessed | tf_op | source)
XLA Modules:
  0.0 406.3 jit_solution(8252731744629288146)
XLA Ops:
  7.2 4.1 %fusion.4 = f32[256,256]{1,0:T(8,128)} fusion(f32[1024,256]{1,0:T(8,128)} %orb_ref.1), kind=kOutput, calls=%fused_computation.20 | convolution fusion | flops 805306368 | bytes 1310720 | tf_op jit(solution)/shard_map/dot_general | solution.py:23
  11.4 0.1 pad_add_fusion
  11.5 0.7 broadcast_subtract_fusion.index_ref
  12.2 12.5 %mode_first.1 = f32[512,256]{1,0:T(8,128)} custom-call(s32[4,8]{1,0:T(4,128)} %broadcast_subtract_fusion.index_ref, f32[8,64,4096]{2,1,0:T(8,128)} %x_ref.3, f32[1024,256]{1,0:T(8,128)} %orb_ref.1, f32[512,256]{1,0:T(8,128)} %nu_ref.3), custom_call_target="tpu_custom_call" | custom-call | tf_op jit(solution)/shard_map/mode_first/pallas_call | solution.py:238
  24.7 0.7 convert_bitcast_fusion
  25.4 0.1 broadcast_select_fusion
  25.5 13.5 %psum.42 = f32[4,8]{1,0:T(4,128)S(1)} all-reduce(f32[4,8]{1,0:T(4,128)S(1)} %broadcast_select_fusion), channel_id=1, replica_groups=mesh['aux'=8,'orb'=4] {'orb'}, use_global_device_ids=true, to_apply=%region_0.1 | all-reduce | flops 32 | bytes 256 | tf_op jit(solution)/shard_map/psum | solution.py:234
  39.0 0.7 reshape.20.at_ref
  39.6 1.0 convolution_multiply_fusion.right_ref
  40.7 9.2 %all-reduce.6.cloned.1.call-done = f32[256,256]{1,0:T(8,128)} async-done(((f32[256,256]{1,0:T(8,128)}), f32[256,256]{1,0:T(8,128)}) %all-reduce.6.cloned.1.call-update) | async-done | bytes 262160 | tf_op jit(solution)/shard_map/psum | solution.py:234
  49.8 1.0 broadcast_multiply_fusion.left_ref
  50.8 16.7 %inverse_first.1 = (f32[256,256]{1,0:T(8,128)S(1)}, f32[1,256]{1,0:T(1,128)}) custom-call(f32[256,256]{1,0:T(8,128)S(1)} %broadcast_multiply_fusion.left_ref, f32[256,256]{1,0:T(8,128)S(1)} %convolution_multiply_fusion.right_ref), custom_call_target="tpu_custom_call" | custom-call | flops 1000000000 | bytes 1048576 | tf_op jit(solution)/shard_map/inverse_first/pallas_call | solution.py:199
  67.6 0.7 copy-done
  68.3 29.6 %all-gather.2.cloned.1.call-done.part_ref = f32[2048,256]{1,0:T(8,128)} async-done(((f32[512,256]{1,0:T(8,128)}), f32[2048,256]{1,0:T(8,128)}) %all-gather.2.cloned.1.call-update) | async-done | bytes 2097168 | tf_op jit(solution)/shard_map/all_gather | solution.py:249
  97.8 11.9 %solve_first.1 = (f32[2048,256]{1,0:T(8,128)}, f32[256,256]{1,0:T(8,128)}) custom-call(s32[32]{0:T(128)} %reshape.20.at_ref, f32[2048,256]{1,0:T(8,128)} %all-gather.2.cloned.1.call-done.part_ref, f32[256,256]{1,0:T(8,128)} %copy-done), custom_call_target="tpu_custom_call" | custom-call | tf_op jit(solution)/shard_map/solve_first/pallas_call | solution.py:253
  109.9 16.9 %mode_second.1 = (f32[8,4096,256]{2,1,0:T(8,128)}, f32[1024,256]{1,0:T(8,128)}) custom-call(s32[4,8]{1,0:T(4,128)} %broadcast_subtract_fusion.index_ref, f32[8,64,4096]{2,1,0:T(8,128)} %x_ref.3, f32[2048,256]{1,0:T(8,128)} %get-tuple-element.12.a_ref, f32[512,256]{1,0:T(8,128)} %nu_ref.3), custom_call_target="tpu_custom_call" | custom-call | tf_op jit(solution)/shard_map/mode_second/pallas_call | solution.py:266
  126.8 35.7 %all-reduce.8.cloned.1.call-done.left_ref.right_ref = f32[256,256]{1,0:T(8,128)} async-done(((f32[256,256]{1,0:T(8,128)}), f32[256,256]{1,0:T(8,128)}) %all-reduce.8.cloned.1.call-update) | async-done | bytes 262160 | tf_op jit(solution)/shard_map/psum | solution.py:264
  162.5 1.1 select_reduce_fusion
  163.6 2.3 broadcast_divide_fusion.2
  165.9 16.9 %inverse_second.1 = (f32[256,256]{1,0:T(8,128)S(1)}, f32[1,256]{1,0:T(1,128)}) custom-call(f32[256,256]{1,0:T(8,128)S(1)} %copy-done.1, f32[256,256]{1,0:T(8,128)S(1)} %convolution_multiply_fusion.right_ref), custom_call_target="tpu_custom_call" | custom-call | flops 1000000000 | bytes 1048576 | tf_op jit(solution)/shard_map/inverse_second/pallas_call | solution.py:199
  182.8 39.6 %all-reduce.10.cloned.1.call-done = f32[1024,256]{1,0:T(8,128)} async-done(((f32[1024,256]{1,0:T(8,128)}), f32[1024,256]{1,0:T(8,128)}) %all-reduce.10.cloned.1.call-update) | async-done | bytes 1048592 | tf_op jit(solution)/shard_map/psum | solution.py:285
  222.4 2.2 fusion.5.b_ref
  224.7 2.5 fusion.6
  227.3 1.5 broadcast_divide_fusion
  228.8 14.2 %mode_third.1 = f32[512,256]{1,0:T(8,128)} custom-call(s32[4,8]{1,0:T(4,128)} %broadcast_subtract_fusion.index_ref, f32[8,4096,256]{2,1,0:T(8,128)} %get-tuple-element.17.e_ref, f32[1024,256]{1,0:T(8,128)} %copy-done.3), custom_call_target="tpu_custom_call" | custom-call | tf_op jit(solution)/shard_map/mode_third/pallas_call | solution.py:291
  243.0 19.2 %all-reduce.12.cloned.1.call-done.left_ref = f32[256,256]{1,0:T(8,128)} async-done(((f32[256,256]{1,0:T(8,128)}), f32[256,256]{1,0:T(8,128)}) %all-reduce.12.cloned.1.call-update) | async-done | bytes 262160 | tf_op jit(solution)/shard_map/psum | solution.py:289
  262.2 0.9 copy-done.2
  263.2 16.5 %inverse_third.1 = (f32[256,256]{1,0:T(8,128)S(1)}, f32[1,256]{1,0:T(1,128)S(1)}) custom-call(f32[256,256]{1,0:T(8,128)S(1)} %copy-done.2, f32[256,256]{1,0:T(8,128)S(1)} %copy-done.1), custom_call_target="tpu_custom_call" | custom-call | flops 1000000000 | bytes 1048576 | tf_op jit(solution)/shard_map/inverse_third/pallas_call | solution.py:199
  279.7 1.0 broadcast_divide_fusion.1
  280.7 116.2 %all-reduce.14.cloned.1.call-done = f32[512,256]{1,0:T(8,128)} async-done(((f32[512,256]{1,0:T(8,128)}), f32[512,256]{1,0:T(8,128)}) %all-reduce.14.cloned.1.call-update) | async-done | bytes 524304 | tf_op jit(solution)/shard_map/psum | solution.py:305
  397.0 1.6 multiply_reduce_fusion
  398.6 0.8 broadcast_divide_fusion.3
  (32 shorter events, 0.4 us)
Async XLA Ops:
  7.2 4.3 %copy-start.7 = (s32[4,8]{1,0:T(4,128)S(1)}, s32[4,8]{1,0:T(4,128)}, u32[]{:S(2)}) copy-start(s32[4,8]{1,0:T(4,128)} %param.5) | copy-start | bytes 388
  7.2 42.7 %all-reduce.6.cloned.1.call-start = ((), (), s32[]{:S(2)}) async-start(), calls=%async_computation.1 | async-start | bytes 524288 | tf_op jit(solution)/shard_map/psum | solution.py:234
  11.4 86.5 %all-gather.2.cloned.1.call-start = ((), (), s32[]{:S(2)}) async-start(), calls=%async_computation | async-start | bytes 2621440 | tf_op jit(solution)/shard_map/all_gather | solution.py:249
  12.2 27.5 %copy-start.5 = (f32[512,256]{1,0:T(8,128)S(1)}, f32[512,256]{1,0:T(8,128)}, u32[]{:S(2)}) copy-start(f32[512,256]{1,0:T(8,128)} %nu_ref.3) | copy-start | bytes 1572868
  24.7 137.8 %all-reduce.8.cloned.1.call-start = ((), (), s32[]{:S(2)}) async-start(), calls=%async_computation.2 | async-start | bytes 524288 | tf_op jit(solution)/shard_map/psum | solution.py:264
  67.6 0.7 copy-start
  109.8 112.6 %all-reduce.10.cloned.1.call-start = ((), (), s32[]{:S(2)}) async-start(), calls=%async_computation.3 | async-start | bytes 2097152 | tf_op jit(solution)/shard_map/psum | solution.py:285
  162.5 3.4 copy-start.1
  165.9 96.4 %all-reduce.12.cloned.1.call-start = ((), (), s32[]{:S(2)}) async-start(), calls=%async_computation.4 | async-start | bytes 524288 | tf_op jit(solution)/shard_map/psum | solution.py:289
  224.6 4.1 %copy-start.3 = (f32[1024,256]{1,0:T(8,128)}, f32[1024,256]{1,0:T(8,128)S(1)}, u32[]{:S(2)}) copy-start(f32[1024,256]{1,0:T(8,128)S(1)} %fusion.5.b_ref) | copy-start | bytes 3145732
  224.7 2.6 copy-start.6
  227.2 169.7 %all-reduce.14.cloned.1.call-start = ((), (), s32[]{:S(2)}) async-start(), calls=%async_computation.5 | async-start | bytes 1048576 | tf_op jit(solution)/shard_map/psum | solution.py:305
  262.2 0.9 copy-start.2
  263.2 16.5 %copy-start.4 = (f32[1024,256]{1,0:T(8,128)S(1)}, f32[1024,256]{1,0:T(8,128)}, u32[]{:S(2)}) copy-start(f32[1024,256]{1,0:T(8,128)} %copy-done.3) | copy-start | bytes 3145732
Sparse Core Ops, SparseCore 0:
  11.5 38.3 all-reduce.5
  52.0 45.8 all-gather.1
  109.9 52.4 all-reduce.7
  166.1 56.3 all-reduce.9
  227.3 34.8 all-reduce.11
  267.9 128.9 all-reduce.13

commit v2 on v1

--- a/solution.py
+++ b/solution.py
@@ -17,6 +17,87 @@
 f32 = jnp.float32
 bf16 = jnp.bfloat16
 PANEL = 32
+
+
+MESH = pl.DeviceIdType.MESH
+
+
+def reduce_kernel(steps, x_ref, out_ref, sum_ref, all_ref, *scratch):
+    count = len(steps)
+    landing = scratch[:count]
+    send_sem, recv_sem = scratch[count:]
+    bits, partners = [], []
+    for axis, bit in steps:
+        here = lax.axis_index(axis)
+        value = (here // (1 << bit)) % 2
+        bits.append(value)
+        partners.append({axis: here + (1 - 2 * value) * (1 << bit)})
+    barrier = pltpu.get_barrier_semaphore()
+    for partner in partners:
+        pl.semaphore_signal(barrier, inc=1, device_id=partner, device_id_type=MESH)
+    pl.semaphore_wait(barrier, count)
+    sum_ref[...] = x_ref[...]
+    length = sum_ref.shape[0]
+    start = jnp.int32(0)
+    kept = []
+    for step in range(count):
+        length //= 2
+        mine = pl.multiple_of(start + bits[step] * length, 8)
+        other = pl.multiple_of(start + (1 - bits[step]) * length, 8)
+        copy = pltpu.make_async_remote_copy(
+            src_ref=sum_ref.at[pl.ds(other, length), :],
+            dst_ref=landing[step],
+            send_sem=send_sem.at[step],
+            recv_sem=recv_sem.at[step],
+            device_id=partners[step],
+            device_id_type=MESH,
+        )
+        copy.start()
+        copy.wait()
+        sum_ref[pl.ds(mine, length), :] += landing[step][...]
+        start = mine
+        kept.append((mine, length))
+    mine, length = kept[-1]
+    all_ref[pl.ds(mine, length), :] = sum_ref[pl.ds(mine, length), :]
+    for step in reversed(range(count)):
+        mine, length = kept[step]
+        rows = all_ref.at[pl.ds(mine, length), :]
+        copy = pltpu.make_async_remote_copy(
+            src_ref=rows,
+            dst_ref=rows,
+            send_sem=send_sem.at[count + step],
+            recv_sem=recv_sem.at[count + step],
+            device_id=partners[step],
+            device_id_type=MESH,
+        )
+        copy.start()
+        copy.wait()
+    out_ref[...] = all_ref[...]
+
+
+def all_reduce(x, axes, number, name):
+    steps = []
+    for axis in axes:
+        size = lax.axis_size(axis)
+        if size & (size - 1):
+            return lax.psum(x, axes)
+        steps += [(axis, bit) for bit in range(size.bit_length() - 1)]
+    rows, columns = x.shape
+    if rows % (8 << len(steps)):
+        return lax.psum(x, axes)
+    count = len(steps)
+    vmem = pl.BlockSpec(memory_space=pltpu.VMEM)
+    return pl.pallas_call(
+        functools.partial(reduce_kernel, tuple(steps)),
+        out_shape=jax.ShapeDtypeStruct(x.shape, f32),
+        in_specs=[vmem],
+        out_specs=vmem,
+        scratch_shapes=[pltpu.VMEM((rows, columns), f32)] * 2
+        + [pltpu.VMEM((rows >> (step + 1), columns), f32) for step in range(count)]
+        + [pltpu.SemaphoreType.DMA((2 * count,)), pltpu.SemaphoreType.DMA((2 * count,))],
+        compiler_params=pltpu.CompilerParams(collective_id=number, has_side_effects=True),
+        name=name,
+    )(x)
 
 
 def gram_of(matrix):
@@ -231,9 +312,10 @@
     own_row = lax.broadcasted_iota(jnp.int32, (orb_size, slots), 0) == lax.axis_index("orb")
     own_at = jnp.where(own_row, index[0].astype(f32)[None], 0.0)
     s_nu = gram_of(nu_factor) / NU
-    gram_orb, slot_at = lax.psum((gram_of(orb_factor), own_at), "orb")
-    s_orb = gram_orb / MU
-    slot_at = slot_at.astype(jnp.int32).reshape(-1)
+    table = jnp.pad(own_at, ((0, -orb_size % 8), (0, rank - slots)))
+    joined = lax.psum(jnp.concatenate([gram_of(orb_factor), table], axis=0), "orb")
+    s_orb = joined[:rank] / MU
+    slot_at = joined[rank:rank + orb_size, :slots].astype(jnp.int32).reshape(-1)
 
     parts = pl.pallas_call(
         functools.partial(first_kernel, edge),
@@ -261,7 +343,7 @@
         scratch_shapes=[pltpu.VMEM((first_rows, rank), f32)],
         name="solve_first",
     )(slot_at, gathered, inverse_first)
-    gram_a = lax.psum(gram_a, "aux")
+    gram_a = all_reduce(gram_a, ("aux",), 1, "sum_gram_first")
 
     e_all, partial_second = pl.pallas_call(
         functools.partial(second_kernel, edge),
@@ -282,11 +364,11 @@
     )(index, tiles, a_new, nu_factor)
     sums_first = jnp.sum(jnp.where(eye_mask(rank), gram_a, 0.0), axis=0)
     scale_first = jnp.sqrt(sums_first / P_SIZE + epsilon)
-    second_sums = lax.psum(partial_second / scale_first, "aux")
+    second_sums = all_reduce(partial_second / scale_first, ("aux",), 2, "sum_second")
     inverse_second, _ = inverse_of(gram_a, s_nu, P_SIZE, 0, "inverse_second")
     aux_factor = a_new / scale_first
     b_new = jnp.dot(second_sums, inverse_second, precision=highest, preferred_element_type=f32)
-    gram_b = lax.psum(gram_of(b_new), "orb")
+    gram_b = all_reduce(gram_of(b_new), ("orb",), 3, "sum_gram_second")
 
     partial_third = pl.pallas_call(
         functools.partial(third_kernel, edge),
@@ -302,7 +384,7 @@
         ),
         name="mode_third",
     )(index, e_all, b_new)
-    third_sums = lax.psum(partial_third, ("aux", "orb"))
+    third_sums = all_reduce(partial_third, ("aux", "orb"), 4, "sum_third")
     inverse_third, scale_second = inverse_of(gram_b, gram_a, MU, P_SIZE, "inverse_third")
     orb_updated = b_new / scale_second
     c_new = jnp.dot(

time: 407 us -> 299 us (0.73)
  waiting for transfers between devices: 250 us -> 53.5 us
  Pallas kernels: 106 us -> 206 us
  blocking collectives: 13.5 us -> 0 us
    psum x5 -> x1, waiting for transfers between devices: 220 us -> 25 us  [per_device(): lax.psum(jnp.concatenate([gram_of(orb_factor), table], axis=0), 'orb')]
    pallas_call x0 -> x4, Pallas kernels: none -> 100 us  [all_reduce(): pl.pallas_call(functools.partial(reduce_kernel, tuple(steps)), out_shape=...]
    psum x1 -> x0, blocking collectives: 13.5 us -> none  [per_device(): gram_orb, slot_at = lax.psum((gram_of(orb_factor), own_at), 'orb')]
  transfers between devices with their start and end apart: 6 -> 2, of which waited for: 6 -> 2; matrix products, arithmetic and copies ran while one was open for 2% -> 1% of each run, Pallas kernels for 23% -> 10%
where the time goes in v2:
time: 299 us; the launch traced here: 297 us
  Pallas kernels  206 us (69%)
  waiting for transfers between devices  53.5 us (18%)
  between operations  14.2 us (5%)
  matrix products  10.9 us (4%)
  other arithmetic  9.92 us (3%)
  local copies, waits for them, and re-layouts  3.22 us (1%)
    pallas_call x4, Pallas kernels, all_reduce(): pl.pallas_call(functools.partial(reduce_kernel, tuple(steps)), out_shape=...  100 us
    pallas_call x3, Pallas kernels, inverse_of(): pl.pallas_call(functools.partial(inverse_kernel, left_rows, right_rows),...  50.1 us
    all_gather x1, waiting for transfers between devices, per_device(): gathered = lax.all_gather(parts, 'orb', axis=0, tiled=True)  28.4 us
    psum x1, waiting for transfers between devices, per_device(): lax.psum(jnp.concatenate([gram_of(orb_factor), table], axis=0), 'orb')  25 us
    pallas_call x1, Pallas kernels, per_device(): pl.pallas_call(functools.partial(second_kernel, edge), out_shape=(jax.Sha...  16.9 us
    pallas_call x1, Pallas kernels, per_device(): pl.pallas_call(functools.partial(third_kernel, edge), out_shape=jax.Shape...  14.1 us
    pallas_call x1, Pallas kernels, per_device(): pl.pallas_call(functools.partial(first_kernel, edge), out_shape=jax.Shape...  12.3 us
    pallas_call x1, Pallas kernels, per_device(): pl.pallas_call(functools.partial(solve_kernel, edge, blocks), out_shape=(...  11.9 us
  transfers between devices with their start and end apart: 2, of which 2 were waited for; matrix products, arithmetic and copies ran while one was open for 1% of the time, Pallas kernels for 10%

profile of v2, /device:TPU:0, one launch (start us, length us, event | category | flops | bytes accessed | tf_op | source)
XLA Modules:
  0.0 297.4 jit_solution(14746421457712351284)
XLA Ops:
  7.2 0.1 pad_add_fusion
  7.3 0.8 broadcast_subtract_fusion.index_ref
  8.1 3.4 %fusion.4 = f32[256,256]{1,0:T(8,128)S(1)} fusion(f32[1024,256]{1,0:T(8,128)} %orb_ref.1), kind=kOutput, calls=%fused_computation.23 | convolution fusion | flops 805306368 | bytes 1310720 | tf_op jit(solution)/shard_map/dot_general | solution.py:104
  11.6 0.7 select_maximum_fusion
  12.4 12.3 %mode_first.1 = f32[512,256]{1,0:T(8,128)} custom-call(s32[4,8]{1,0:T(4,128)} %copy-done.7, f32[8,64,4096]{2,1,0:T(8,128)} %x_ref.3, f32[1024,256]{1,0:T(8,128)} %orb_ref.1, f32[512,256]{1,0:T(8,128)} %nu_ref.3), custom_call_target="tpu_custom_call" | custom-call | tf_op jit(solution)/shard_map/mode_first/pallas_call | solution.py:320
  24.7 1.0 convolution_multiply_fusion.right_ref
  25.7 25.0 %all-reduce.3.cloned.1.call-done = f32[264,256]{1,0:T(8,128)} async-done(((f32[264,256]{1,0:T(8,128)}), f32[264,256]{1,0:T(8,128)}) %all-reduce.3.cloned.1.call-update) | async-done | bytes 270352 | tf_op jit(solution)/shard_map/psum | solution.py:316
  50.7 0.7 slice_convert_fusion
  51.4 0.6 reshape.20.at_ref
  52.0 1.0 slice_multiply_fusion.left_ref
  53.0 16.7 %inverse_first.1 = (f32[256,256]{1,0:T(8,128)S(1)}, f32[1,256]{1,0:T(1,128)}) custom-call(f32[256,256]{1,0:T(8,128)S(1)} %slice_multiply_fusion.left_ref, f32[256,256]{1,0:T(8,128)S(1)} %convolution_multiply_fusion.right_ref), custom_call_target="tpu_custom_call" | custom-call | flops 1000000000 | bytes 1048576 | tf_op jit(solution)/shard_map/inverse_first/pallas_call | solution.py:280
  69.7 0.7 copy-done.2
  70.4 28.4 %all-gather.2.cloned.1.call-done.part_ref = f32[2048,256]{1,0:T(8,128)} async-done(((f32[512,256]{1,0:T(8,128)}), f32[2048,256]{1,0:T(8,128)}) %all-gather.2.cloned.1.call-update) | async-done | bytes 2097168 | tf_op jit(solution)/shard_map/all_gather | solution.py:331
  98.9 11.9 %solve_first.1 = (f32[2048,256]{1,0:T(8,128)}, f32[256,256]{1,0:T(8,128)}) custom-call(s32[32]{0:T(128)} %reshape.20.at_ref, f32[2048,256]{1,0:T(8,128)} %all-gather.2.cloned.1.call-done.part_ref, f32[256,256]{1,0:T(8,128)} %copy-done.2), custom_call_target="tpu_custom_call" | custom-call | tf_op jit(solution)/shard_map/solve_first/pallas_call | solution.py:335
  110.8 18.0 %sum_gram_first.1.left_ref.right_ref = f32[256,256]{1,0:T(8,128)} custom-call(f32[256,256]{1,0:T(8,128)} %get-tuple-element.13.x_ref), custom_call_target="tpu_custom_call" | custom-call | tf_op jit(solution)/shard_map/sum_gram_first/pallas_call | solution.py:90
  128.8 1.0 select_reduce_fusion
  129.8 0.9 copy-done
  130.7 16.9 %inverse_second.1 = (f32[256,256]{1,0:T(8,128)S(1)}, f32[1,256]{1,0:T(1,128)}) custom-call(f32[256,256]{1,0:T(8,128)S(1)} %copy-done, f32[256,256]{1,0:T(8,128)S(1)} %convolution_multiply_fusion.right_ref), custom_call_target="tpu_custom_call" | custom-call | flops 1000000000 | bytes 1048576 | tf_op jit(solution)/shard_map/inverse_second/pallas_call | solution.py:280
  147.6 16.9 %mode_second.1 = (f32[8,4096,256]{2,1,0:T(8,128)}, f32[1024,256]{1,0:T(8,128)}) custom-call(s32[4,8]{1,0:T(4,128)} %copy-done.7, f32[8,64,4096]{2,1,0:T(8,128)} %x_ref.3, f32[2048,256]{1,0:T(8,128)} %get-tuple-element.12.a_ref, f32[512,256]{1,0:T(8,128)} %nu_ref.3), custom_call_target="tpu_custom_call" | custom-call | tf_op jit(solution)/shard_map/mode_second/pallas_call | solution.py:348
  164.5 2.3 broadcast_divide_fusion.2.x_ref
  166.8 29.2 %sum_second.1 = f32[1024,256]{1,0:T(8,128)} custom-call(f32[1024,256]{1,0:T(8,128)} %broadcast_divide_fusion.2.x_ref), custom_call_target="tpu_custom_call" | custom-call | tf_op jit(solution)/shard_map/sum_second/pallas_call | solution.py:90
  196.0 2.3 fusion.5.b_ref
  198.3 2.5 fusion.6.x_ref
  200.8 20.1 %sum_gram_second.1.left_ref = f32[256,256]{1,0:T(8,128)} custom-call(f32[256,256]{1,0:T(8,128)} %fusion.6.x_ref), custom_call_target="tpu_custom_call" | custom-call | tf_op jit(solution)/shard_map/sum_gram_second/pallas_call | solution.py:90
  221.0 0.9 copy-done.3
  221.9 16.5 %inverse_third.1 = (f32[256,256]{1,0:T(8,128)S(1)}, f32[1,256]{1,0:T(1,128)S(1)}) custom-call(f32[256,256]{1,0:T(8,128)S(1)} %copy-done.3, f32[256,256]{1,0:T(8,128)S(1)} %copy-done.1), custom_call_target="tpu_custom_call" | custom-call | flops 1000000000 | bytes 1048576 | tf_op jit(solution)/shard_map/inverse_third/pallas_call | solution.py:280
  238.4 1.0 broadcast_divide_fusion.1
  239.5 1.5 broadcast_divide_fusion
  240.9 14.1 %mode_third.1.x_ref = f32[512,256]{1,0:T(8,128)} custom-call(s32[4,8]{1,0:T(4,128)} %copy-done.7, f32[8,4096,256]{2,1,0:T(8,128)} %get-tuple-element.17.e_ref, f32[1024,256]{1,0:T(8,128)} %copy-done.4), custom_call_target="tpu_custom_call" | custom-call | tf_op jit(solution)/shard_map/mode_third/pallas_call | solution.py:373
  255.0 33.0 %sum_third.1 = f32[512,256]{1,0:T(8,128)} custom-call(f32[512,256]{1,0:T(8,128)} %mode_third.1.x_ref), custom_call_target="tpu_custom_call" | custom-call | tf_op jit(solution)/shard_map/sum_third/pallas_call | solution.py:90
  288.1 1.6 multiply_reduce_fusion
  289.7 0.8 broadcast_divide_fusion.3
  (24 shorter events, 0.2 us)
Async XLA Ops:
  7.2 43.6 %all-reduce.3.cloned.1.call-start = ((), (), s32[]{:S(2)}) async-start(), calls=%async_computation | async-start | bytes 540672 | tf_op jit(solution)/shard_map/psum | solution.py:316
  8.1 4.3 %copy-start.7 = (s32[4,8]{1,0:T(4,128)}, s32[4,8]{1,0:T(4,128)S(1)}, u32[]{:S(2)}) copy-start(s32[4,8]{1,0:T(4,128)S(1)} %broadcast_subtract_fusion.index_ref) | copy-start | bytes 388
  12.3 12.4 %copy-start.5 = (f32[512,256]{1,0:T(8,128)S(1)}, f32[512,256]{1,0:T(8,128)}, u32[]{:S(2)}) copy-start(f32[512,256]{1,0:T(8,128)} %nu_ref.3) | copy-start | bytes 1572868
  12.3 86.5 %all-gather.2.cloned.1.call-start = ((), (), s32[]{:S(2)}) async-start(), calls=%async_computation.1 | async-start | bytes 2621440 | tf_op jit(solution)/shard_map/all_gather | solution.py:331
  69.7 0.7 copy-start.2
  129.8 0.9 copy-start
  196.0 24.9 %copy-start.1 = (f32[256,256]{1,0:T(8,128)S(1)}, f32[256,256]{1,0:T(8,128)}, u32[]{:S(2)}) copy-start(f32[256,256]{1,0:T(8,128)} %sum_gram_first.1.left_ref.right_ref) | copy-start | bytes 786436
  198.3 40.1 %copy-start.4 = (f32[1024,256]{1,0:T(8,128)}, f32[1024,256]{1,0:T(8,128)S(1)}, u32[]{:S(2)}) copy-start(f32[1024,256]{1,0:T(8,128)S(1)} %fusion.5.b_ref) | copy-start | bytes 3145732
  221.0 1.0 copy-start.3
  221.9 17.5 %copy-start.6 = (f32[2048,256]{1,0:T(8,128)S(1)}, f32[2048,256]{1,0:T(8,128)}, u32[]{:S(2)}) copy-start(f32[2048,256]{1,0:T(8,128)} %get-tuple-element.12.a_ref) | copy-start | bytes 6291460
Sparse Core Ops, SparseCore 0:
  12.4 38.2 all-reduce.2
  52.9 45.9 all-gather.1
